TPU v7x, 256 devices: a whole 4x4x8 slice. The times are simulated.
256 devices in a mesh: expert: 32 (over y, x, core), dp: 8 (over z).
Axes of the slice: x: 4, y: 4, z: 8, core: 2. Of those that a mesh axis runs over, the one named last changes fastest.
Arguments:
- tokens: bfloat16 [32768, 2048], P(('expert', 'dp')), may hold values from -6 to 6
- cotangent: bfloat16 [32768, 2048], P(('expert', 'dp')), may hold values from -6 to 6
- routes: int32 [32768, 4], P(('expert', 'dp')), may hold values from 0 to 31, all different within a row; in each aligned block of 128 rows (0 to 127, 128 to 255, ...) at most 24 rows name the same one
- gate_values: bfloat16 [32768, 4], P(('expert', 'dp')), may hold values from 0.099609375 to 1
- w_gate: bfloat16 [32, 2048, 512], P('expert', 'dp'), may hold values from -0.125 to 0.125
- w_up: bfloat16 [32, 2048, 512], P('expert', 'dp'), may hold values from -0.125 to 0.125
- w_down: bfloat16 [32, 512, 2048], P('expert', None, 'dp'), may hold values from -0.25 to 0.25
Outputs:
- token_grad: bfloat16 [32768, 2048], P(('expert', 'dp'))
- gate_weight_grad: bfloat16 [32, 2048, 512], P('expert', 'dp')
- up_weight_grad: bfloat16 [32, 2048, 512], P('expert', 'dp')
- down_weight_grad: bfloat16 [32, 512, 2048], P('expert', None, 'dp')
Inputs may be any that keep to these rules, and one draw needn't show every extreme that they name: `routes`: each row names 4 different experts. Among the rows of one device no expert is named more than 24 times, and some device names some expert exactly 24 times.
All inputs are finite; a program needn't handle non-finite values.
Results may differ from a plain program's by a relative error of at most 0.017.
Values may be sent and summed in bfloat16 or wider, within the bound.
No kernel may reach another device: no remote copies, remote signals or barrier semaphores. Data moves between devices by JAX's collectives and lax.ppermute only.
A program may use at most 128 MiB of HBM per device.

v0:
```python
import jax
import jax.numpy as jnp
from jax import lax
from jax.experimental.layout import Layout, with_layout_constraint
from jax.sharding import PartitionSpec as P


def slot_masks(routes, gate_values, experts, capacity):
    tok_dev = routes.shape[0]
    ids = jnp.arange(experts, dtype=jnp.int32)
    hit = routes[:, :, None] == ids[None, None, :]
    member = jnp.any(hit, axis=1)
    gate = jnp.sum(jnp.where(hit, gate_values.astype(jnp.float32)[:, :, None], 0.0), axis=1)
    row = lax.broadcasted_iota(jnp.int32, (tok_dev, tok_dev), 0)
    col = lax.broadcasted_iota(jnp.int32, (tok_dev, tok_dev), 1)
    earlier = (row < col).astype(jnp.bfloat16)
    before = lax.dot_general(
        member.astype(jnp.bfloat16),
        earlier,
        (((0,), (0,)), ((), ())),
        preferred_element_type=jnp.float32,
    ).astype(jnp.int32)
    rank = jnp.where(member.T, before, -1)
    place = rank[:, None, :] == jnp.arange(capacity, dtype=jnp.int32)[None, :, None]
    place = place.reshape(experts * capacity, tok_dev)
    weight = jnp.broadcast_to(gate.T[:, None, :], (experts, capacity, tok_dev)).reshape(
        experts * capacity, tok_dev
    )
    return (place.astype(jnp.bfloat16), jnp.where(place, weight, 0.0).astype(jnp.bfloat16))


def row_major(a):
    return with_layout_constraint(a, Layout(major_to_minor=(0, 1)))


def matmul(a, b, dims):
    return lax.dot_general(a, b, (dims, ((), ())), preferred_element_type=jnp.float32)


def local(tokens, cotangent, routes, gate_values, w_gate, w_up, w_down):
    experts = lax.axis_size("expert")
    tok_dev, model_width = tokens.shape
    fan_out = routes.shape[1]
    hidden_width = w_gate.shape[2]
    capacity = min(tok_dev, 3 * tok_dev * fan_out // (2 * experts))
    shard = jnp.concatenate([w_gate[0], w_up[0], w_down[0].T], axis=1)
    full = row_major(lax.all_gather(row_major(shard), "dp", axis=0, tiled=True))
    place, weighted = slot_masks(routes, gate_values, experts, capacity)

    def exchange(rows):
        return lax.all_to_all(
            rows.reshape(experts, capacity, model_width),
            "expert",
            split_axis=0,
            concat_axis=0,
            tiled=True,
        ).reshape(experts * capacity, model_width)

    x_rows = exchange(matmul(place, tokens, ((1,), (0,))).astype(jnp.bfloat16))
    scaled = exchange(matmul(weighted, cotangent, ((1,), (0,))).astype(jnp.bfloat16))
    pre = matmul(x_rows, full[:, : 2 * hidden_width], ((1,), (0,)))
    gate_pre = pre[:, :hidden_width]
    up_pre = pre[:, hidden_width:]
    sigmoid_gate = 1.0 / (1.0 + jnp.exp(-gate_pre))
    activated = gate_pre * sigmoid_gate
    hidden = (activated * up_pre).astype(jnp.bfloat16)
    hidden_grad = matmul(scaled, full[:, 2 * hidden_width :], ((1,), (0,)))
    gate_grad = (
        hidden_grad * up_pre * sigmoid_gate * (1.0 + gate_pre * (1.0 - sigmoid_gate))
    ).astype(jnp.bfloat16)
    up_grad = (hidden_grad * activated).astype(jnp.bfloat16)
    both_grad = jnp.concatenate([gate_grad, up_grad], axis=1)
    in_term = matmul(x_rows, both_grad, ((0,), (0,))).astype(jnp.bfloat16)
    down_term = matmul(scaled, hidden, ((0,), (0,))).astype(jnp.bfloat16)
    terms = jnp.concatenate([in_term, down_term], axis=1)
    sums = row_major(lax.psum_scatter(row_major(terms), "dp", scatter_dimension=0, tiled=True))
    row_grad = matmul(both_grad, full[:, : 2 * hidden_width], ((1,), (1,)))
    returned = exchange(row_grad.astype(jnp.bfloat16))
    token_grad = matmul(place, returned, ((0,), (0,))).astype(jnp.bfloat16)
    return (
        token_grad,
        sums[None, :, :hidden_width],
        sums[None, :, hidden_width : 2 * hidden_width],
        sums[:, 2 * hidden_width :].T[None],
    )


def solution(mesh):
    in_specs = (
        P(("expert", "dp"), None),
        P(("expert", "dp"), None),
        P(("expert", "dp"), None),
        P(("expert", "dp"), None),
        P("expert", "dp", None),
        P("expert", "dp", None),
        P("expert", None, "dp"),
    )
    out_specs = (
        P(("expert", "dp"), None),
        P("expert", "dp", None),
        P("expert", "dp", None),
        P("expert", None, "dp"),
    )
    return jax.shard_map(local, mesh=mesh, in_specs=in_specs, out_specs=out_specs, check_vma=False)
```

profile of v0, /device:TPU:1, one launch (start us, length us, event | category | flops | bytes accessed | tf_op | source)
XLA Modules:
  0.0 214.0 jit_solution(319687289944547735)
XLA Ops:
  7.2 0.0 copy-start
  7.2 0.0 all-gather.2.cloned.1.call-start
  7.2 1.1 copy.38
  8.4 2.0 pad_maximum_fusion.4
  10.4 0.0 all-gather.2.cloned.1.call-update
  10.4 0.1 eq.45
  10.5 0.7 fusion.15
  11.2 0.1 fusion.11
  11.3 0.2 bitcast_compare_fusion
  11.5 0.0 copy-done
  11.5 2.6 %convolution_convert_fusion.1 = bf16[768,2048]{1,0:T(8,128)(2,1)} fusion(pred[768,128]{1,0:T(32,128)(4,1)S(1)} %bitcast_compare_fusion, bf16[128,2048]{1,0:T(8,128)(2,1)S(1)} %copy-done), kind=kOutput, calls=%fused_computation.7 | convolution fusion | flops 404226048 | bytes 3768320 | tf_op jit(solution)/shard_map/dot_general | solution.py:37
  14.1 8.8 %all-to-all-start.1 = ((bf16[32,24,2048]{2,1,0:T(8,128)(2,1)}), bf16[32,24,2048]{2,1,0:T(8,128)(2,1)}, u32[]{:S(2)}, u32[]{:S(2)}) async-start(bf16[32,24,2048]{2,1,0:T(8,128)(2,1)} %bitcast.43), calls=%async_computation.1 | async-start | bytes 6291456 | tf_op jit(solution)/shard_map/all_to_all | solution.py:51
  22.9 0.0 copy-done.3
  23.0 0.2 fusion.12
  23.1 2.6 %convolution_convert_fusion.2 = bf16[768,2048]{1,0:T(8,128)(2,1)} fusion(bf16[768,128]{1,0:T(8,128)(2,1)S(1)} %fusion.12, bf16[128,2048]{1,0:T(8,128)(2,1)S(1)} %copy-done.1), kind=kOutput, calls=%fused_computation.8 | convolution fusion | flops 404226048 | bytes 3866624 | tf_op jit(solution)/shard_map/dot_general | solution.py:37
  25.7 36.4 %all-to-all-done.1 = bf16[32,24,2048]{2,1,0:T(8,128)(2,1)} async-done(((bf16[32,24,2048]{2,1,0:T(8,128)(2,1)}), bf16[32,24,2048]{2,1,0:T(8,128)(2,1)}, u32[]{:S(2)}, u32[]{:S(2)}) %all-to-all-start.1) | async-done | bytes 3145760 | tf_op jit(solution)/shard_map/all_to_all | solution.py:51
  62.1 7.3 %all-to-all-start = ((bf16[32,24,2048]{2,1,0:T(8,128)(2,1)}), bf16[32,24,2048]{2,1,0:T(8,128)(2,1)}, u32[]{:S(2)}, u32[]{:S(2)}) async-start(bf16[32,24,2048]{2,1,0:T(8,128)(2,1)} %bitcast.44), calls=%async_computation | async-start | bytes 6291456 | tf_op jit(solution)/shard_map/all_to_all | solution.py:51
  69.4 0.0 reduce-scatter.2.cloned.1.call-start
  69.4 19.5 %all-gather.2.cloned.1.call-done = bf16[2048,1536]{1,0:T(8,128)(2,1)} async-done(((bf16[256,1536]{1,0:T(8,128)(2,1)}), bf16[2048,1536]{1,0:T(8,128)(2,1)}) %all-gather.2.cloned.1.call-update) | async-done | bytes 6291472 | tf_op jit(solution)/shard_map/all_gather | solution.py:47
  88.9 8.3 %fusion.2 = f32[768,1024]{0,1:T(8,128)} fusion(bf16[768,2048]{1,0:T(8,128)(2,1)} %bitcast.11, bf16[2048,1536]{1,0:T(8,128)(2,1)} %all-gather.2.cloned.1.call-done), kind=kOutput, calls=%fused_computation.4 | convolution fusion | flops 3221225472 | bytes 10485760 | tf_op jit(solution)/shard_map/dot_general | solution.py:37
  97.2 11.5 %all-to-all-done = bf16[32,24,2048]{2,1,0:T(8,128)(2,1)} async-done(((bf16[32,24,2048]{2,1,0:T(8,128)(2,1)}), bf16[32,24,2048]{2,1,0:T(8,128)(2,1)}, u32[]{:S(2)}, u32[]{:S(2)}) %all-to-all-start) | async-done | bytes 3145760 | tf_op jit(solution)/shard_map/all_to_all | solution.py:51
  108.7 4.9 %convolution_convert_fusion.3 = bf16[2048,512]{1,0:T(8,128)(2,1)S(1)} fusion(bf16[768,2048]{1,0:T(8,128)(2,1)} %bitcast.5, f32[768,1024]{0,1:T(8,128)} %fusion.2), kind=kOutput, calls=%fused_computation.9 | convolution fusion | flops 1614020608 | bytes 8388608 | tf_op jit(solution)/shard_map/dot_general | solution.py:37
  113.6 4.9 %multiply_convert_fusion.2 = (bf16[768,512]{0,1:T(8,128)(2,1)S(1)}, bf16[768,512]{0,1:T(8,128)(2,1)S(1)}) fusion(f32[768,1024]{0,1:T(8,128)S(1)} %copy-done.4, bf16[768,2048]{1,0:T(8,128)(2,1)} %bitcast.5, bf16[2048,1536]{1,0:T(8,128)(2,1)} %all-gather.2.cloned.1.call-done), kind=kOutput, calls=%fused_computation.17 | convolution fusion | flops 1615724544 | bytes 9961472 | tf_op jit(solution)/shard_map/dot_general | solution.py:37
  118.6 6.7 %convolution_convert_fusion = bf16[2048,1024]{1,0:T(8,128)(2,1)S(1)} fusion(bf16[768,2048]{1,0:T(8,128)(2,1)} %bitcast.11, bf16[768,512]{0,1:T(8,128)(2,1)S(1)} %get-tuple-element.21, bf16[768,512]{0,1:T(8,128)(2,1)S(1)} %get-tuple-element.20), kind=kOutput, calls=%fused_computation.1 | convolution fusion | flops 3226468352 | bytes 8912896 | tf_op jit(solution)/shard_map/dot_general | solution.py:37
  125.3 3.2 %pad_maximum_fusion = bf16[2048,1536]{1,0:T(8,128)(2,1)} fusion(bf16[2048,512]{1,0:T(8,128)(2,1)S(1)} %convolution_convert_fusion.3, bf16[2048,1024]{1,0:T(8,128)(2,1)S(1)} %convolution_convert_fusion), kind=kLoop, calls=%fused_computation | loop fusion | flops 12582912 | bytes 12582912 | tf_op jit(solution)/shard_map/concatenate | solution.py:75
  128.5 0.0 reduce-scatter.2.cloned.1.call-update
  128.5 6.0 %fusion.4 = bf16[768,2048]{1,0:T(8,128)(2,1)S(1)} fusion(bf16[2048,1536]{1,0:T(8,128)(2,1)} %all-gather.2.cloned.1.call-done, bf16[768,512]{0,1:T(8,128)(2,1)S(1)} %get-tuple-element.21, bf16[768,512]{0,1:T(8,128)(2,1)S(1)} %get-tuple-element.20), kind=kOutput, calls=%fused_computation.6 | convolution fusion | flops 3225944064 | bytes 8912896 | tf_op jit(solution)/shard_map/dot_general | solution.py:37
  134.5 45.3 %all_to_all.15 = bf16[32,24,2048]{2,1,0:T(8,128)(2,1)S(1)} all-to-all(bf16[32,24,2048]{2,1,0:T(8,128)(2,1)S(1)} %bitcast.45), channel_id=1, replica_groups=mesh['expert'=32,'dp'=8] {'expert'}, dimensions={0} | all-to-all | bytes 6291456 | tf_op jit(solution)/shard_map/all_to_all | solution.py:51
  179.8 1.4 fusion.7
  181.2 23.1 %reduce-scatter.2.cloned.1.call-done = bf16[256,1536]{1,0:T(8,128)(2,1)} async-done(((bf16[2048,1536]{1,0:T(8,128)(2,1)}), bf16[256,1536]{1,0:T(8,128)(2,1)}) %reduce-scatter.2.cloned.1.call-update) | async-done | bytes 786448 | tf_op jit(solution)/shard_map/reduce_scatter | solution.py:76
  204.3 2.0 slice_bitcast_fusion
  206.3 0.8 copy.43
  (10 shorter events, 0.0 us)
Async XLA Ops:
  7.2 4.3 %copy-start = (bf16[128,2048]{1,0:T(8,128)(2,1)S(1)}, bf16[128,2048]{1,0:T(8,128)(2,1)}, u32[]{:S(2)}) copy-start(bf16[128,2048]{1,0:T(8,128)(2,1)} %param.7) | copy-start | bytes 1572868
  7.2 81.7 %all-gather.2.cloned.1.call-start = ((), (), s32[]{:S(2)}) async-start(), calls=%async_computation.4 | async-start | bytes 7077888 | tf_op jit(solution)/shard_map/all_gather | solution.py:47
  14.1 8.8 %copy-start.3 = (bf16[128,4]{0,1:T(4,128)(2,1)S(1)}, bf16[128,4]{0,1:T(4,128)(2,1)}, u32[]{:S(2)}) copy-start(bf16[128,4]{0,1:T(4,128)(2,1)} %param.10) | copy-start | bytes 3076
  14.1 8.8 %copy-start.2 = (s32[128,4]{0,1:T(4,128)S(1)}, s32[128,4]{0,1:T(4,128)}, u32[]{:S(2)}) copy-start(s32[128,4]{0,1:T(4,128)} %param.9) | copy-start | bytes 6148
  14.1 9.0 %copy-start.1 = (bf16[128,2048]{1,0:T(8,128)(2,1)S(1)}, bf16[128,2048]{1,0:T(8,128)(2,1)}, u32[]{:S(2)}) copy-start(bf16[128,2048]{1,0:T(8,128)(2,1)} %param.8) | copy-start | bytes 1572868
  14.1 48.0 %all-to-all-start.1 = ((bf16[32,24,2048]{2,1,0:T(8,128)(2,1)}), bf16[32,24,2048]{2,1,0:T(8,128)(2,1)}, u32[]{:S(2)}, u32[]{:S(2)}) async-start(bf16[32,24,2048]{2,1,0:T(8,128)(2,1)} %bitcast.43), calls=%async_computation.1 | async-start | bytes 6291456 | tf_op jit(solution)/shard_map/all_to_all | solution.py:51
  62.1 46.6 %all-to-all-start = ((bf16[32,24,2048]{2,1,0:T(8,128)(2,1)}), bf16[32,24,2048]{2,1,0:T(8,128)(2,1)}, u32[]{:S(2)}, u32[]{:S(2)}) async-start(bf16[32,24,2048]{2,1,0:T(8,128)(2,1)} %bitcast.44), calls=%async_computation | async-start | bytes 6291456 | tf_op jit(solution)/shard_map/all_to_all | solution.py:51
  69.4 135.0 %reduce-scatter.2.cloned.1.call-start = ((), (), s32[]{:S(2)}) async-start(), calls=%async_computation.5 | async-start | bytes 7077888 | tf_op jit(solution)/shard_map/reduce_scatter | solution.py:76
  108.7 4.9 %copy-start.4 = (f32[768,1024]{0,1:T(8,128)S(1)}, f32[768,1024]{0,1:T(8,128)}, u32[]{:S(2)}) copy-start(f32[768,1024]{0,1:T(8,128)} %fusion.2) | copy-start | bytes 9437188
Sparse Core Ops, SparseCore 0:
  10.5 78.3 all-gather.1
  128.6 75.6 reduce-scatter.1
where the time goes:
time: 214 us
  waiting for transfers between devices  90.5 us (42%)
  blocking collectives  45.3 us (21%)
  matrix products  37.6 us (18%)
  starting transfers between devices  16.1 us (8%)
  between operations  14.2 us (7%)
  other arithmetic  6.23 us (3%)
  local copies, waits for them, and re-layouts  4.04 us (2%)
    all_to_all x2, waiting for transfers between devices, exchange(): lax.all_to_all(rows.reshape(experts, capacity, model_width), 'expert', sp...  47.9 us
    all_to_all x1, blocking collectives, exchange(): lax.all_to_all(rows.reshape(experts, capacity, model_width), 'expert', sp...  45.3 us
    dot_general x8, matrix products, matmul(): lax.dot_general(a, b, (dims, ((), ())), preferred_element_type=jnp.float32)  37.5 us
    reduce_scatter x1, waiting for transfers between devices, local(): lax.psum_scatter(row_major(terms), 'dp', scatter_dimension=0, tiled=True)  23.1 us
    all_gather x1, waiting for transfers between devices, local(): full = row_major(lax.all_gather(row_major(shard), 'dp', axis=0, tiled=True))  19.5 us
    all_to_all x2, starting transfers between devices, exchange(): lax.all_to_all(rows.reshape(experts, capacity, model_width), 'expert', sp...  16 us
  transfers between devices with their start and end apart: 4, of which 4 were waited for; matrix products, arithmetic and copies ran while one was open for 10% of the time, Pallas kernels for 0%

commit v1 on v0

--- a/solution.py
+++ b/solution.py
@@ -44,7 +44,11 @@
     hidden_width = w_gate.shape[2]
     capacity = min(tok_dev, 3 * tok_dev * fan_out // (2 * experts))
     shard = jnp.concatenate([w_gate[0], w_up[0], w_down[0].T], axis=1)
-    full = row_major(lax.all_gather(row_major(shard), "dp", axis=0, tiled=True))
+    full = row_major(
+        jnp.concatenate(
+            lax.all_to_all(jnp.stack([row_major(shard)] * lax.axis_size("dp")), "dp", 0, 0), axis=0
+        )
+    )
     place, weighted = slot_masks(routes, gate_values, experts, capacity)
 
     def exchange(rows):

time: 214 us -> 357 us (1.67)
  waiting for transfers between devices: 90.5 us -> 225 us
  starting transfers between devices: 16.1 us -> 23.6 us
    all_to_all x0 -> x1, waiting for transfers between devices: none -> 139 us  [local(): lax.all_to_all(jnp.stack([row_major(shard)] * lax.axis_size('dp')), 'dp',...]
    all_to_all x2, waiting for transfers between devices: 47.9 us -> 69.7 us  [exchange(): lax.all_to_all(rows.reshape(experts, capacity, model_width), 'expert', sp...]
    all_gather x1 -> x0, waiting for transfers between devices: 19.5 us -> none  [local(): full = row_major(lax.all_gather(row_major(shard), 'dp', axis=0, tiled=True))]
    all_to_all x0 -> x1, starting transfers between devices: none -> 8.32 us  [local(): lax.all_to_all(jnp.stack([row_major(shard)] * lax.axis_size('dp')), 'dp',...]
    reduce_scatter x1, waiting for transfers between devices: 23.1 us -> 16.5 us  [local(): lax.psum_scatter(row_major(terms), 'dp', scatter_dimension=0, tiled=True)]
  transfers between devices with their start and end apart: 4 -> 4, of which waited for: 4 -> 4; matrix products, arithmetic and copies ran while one was open for 10% -> 5% of each run, Pallas kernels for 0% -> 0%
where the time goes in v1:
time: 357 us; the launch traced here: 356 us
  waiting for transfers between devices  225 us (63%)
  blocking collectives  45.3 us (13%)
  matrix products  37.6 us (11%)
  starting transfers between devices  23.6 us (7%)
  between operations  14.2 us (4%)
  local copies, waits for them, and re-layouts  6.24 us (2%)
  other arithmetic  4.38 us (1%)
    all_to_all x1, waiting for transfers between devices, local(): lax.all_to_all(jnp.stack([row_major(shard)] * lax.axis_size('dp')), 'dp',...  139 us
    all_to_all x2, waiting for transfers between devices, exchange(): lax.all_to_all(rows.reshape(experts, capacity, model_width), 'expert', sp...  69.7 us
    all_to_all x1, blocking collectives, exchange(): lax.all_to_all(rows.reshape(experts, capacity, model_width), 'expert', sp...  45.3 us
    dot_general x8, matrix products, matmul(): lax.dot_general(a, b, (dims, ((), ())), preferred_element_type=jnp.float32)  37.4 us
    reduce_scatter x1, waiting for transfers between devices, local(): lax.psum_scatter(row_major(terms), 'dp', scatter_dimension=0, tiled=True)  16.5 us
    all_to_all x2, starting transfers between devices, exchange(): lax.all_to_all(rows.reshape(experts, capacity, model_width), 'expert', sp...  15.1 us
    all_to_all x1, starting transfers between devices, local(): lax.all_to_all(jnp.stack([row_major(shard)] * lax.axis_size('dp')), 'dp',...  8.32 us
  transfers between devices with their start and end apart: 4, of which 4 were waited for; matrix products, arithmetic and copies ran while one was open for 5% of the time, Pallas kernels for 0%

profile of v1, /device:TPU:1, one launch (start us, length us, event | category | flops | bytes accessed | tf_op | source)
XLA Modules:
  0.0 356.5 jit_solution(2450930485351874938)
XLA Ops:
  7.2 0.0 copy-start
  7.2 0.8 fusion.15
  7.9 0.1 fusion.11
  8.1 0.1 eq.45
  8.2 0.2 bitcast_compare_fusion
  8.3 0.0 copy-done
  8.4 2.6 convolution_convert_fusion.1
  11.0 8.8 %all-to-all-start.2 = ((bf16[32,24,2048]{2,1,0:T(8,128)(2,1)}), bf16[32,24,2048]{2,1,0:T(8,128)(2,1)}, u32[]{:S(2)}, u32[]{:S(2)}) async-start(bf16[32,24,2048]{2,1,0:T(8,128)(2,1)} %bitcast.44), calls=%async_computation.2 | async-start | bytes 6291456 | tf_op jit(solution)/shard_map/all_to_all | solution.py:55
  19.7 0.0 copy-done.2
  19.8 0.1 copy.38
  19.9 0.1 pad_maximum_fusion.4
  20.0 39.0 %all-to-all-done.2 = bf16[32,24,2048]{2,1,0:T(8,128)(2,1)} async-done(((bf16[32,24,2048]{2,1,0:T(8,128)(2,1)}), bf16[32,24,2048]{2,1,0:T(8,128)(2,1)}, u32[]{:S(2)}, u32[]{:S(2)}) %all-to-all-start.2) | async-done | bytes 3145760 | tf_op jit(solution)/shard_map/all_to_all | solution.py:55
  59.0 3.2 stack.2
  62.2 8.3 %all-to-all-start.1 = ((bf16[8,256,1536]{2,1,0:T(8,128)(2,1)}), bf16[8,256,1536]{2,1,0:T(8,128)(2,1)}, u32[]{:S(2)}, u32[]{:S(2)}) async-start(bf16[8,256,1536]{2,1,0:T(8,128)(2,1)} %stack.2), calls=%async_computation.1 | async-start | bytes 12582912 | tf_op jit(solution)/shard_map/all_to_all | solution.py:49
  70.5 0.2 fusion.12
  70.7 2.6 convolution_convert_fusion.2
  73.3 139.0 %all-to-all-done.1 = bf16[8,256,1536]{2,1,0:T(8,128)(2,1)} async-done(((bf16[8,256,1536]{2,1,0:T(8,128)(2,1)}), bf16[8,256,1536]{2,1,0:T(8,128)(2,1)}, u32[]{:S(2)}, u32[]{:S(2)}) %all-to-all-start.1) | async-done | bytes 6291488 | tf_op jit(solution)/shard_map/all_to_all | solution.py:49
  212.3 6.3 %all-to-all-start = ((bf16[32,24,2048]{2,1,0:T(8,128)(2,1)}), bf16[32,24,2048]{2,1,0:T(8,128)(2,1)}, u32[]{:S(2)}, u32[]{:S(2)}) async-start(bf16[32,24,2048]{2,1,0:T(8,128)(2,1)} %bitcast.45), calls=%async_computation | async-start | bytes 6291456 | tf_op jit(solution)/shard_map/all_to_all | solution.py:55
  218.6 0.2 reduce-scatter.2.cloned.1.call-start
  218.8 8.3 %fusion.2 = f32[768,1024]{0,1:T(8,128)} fusion(bf16[768,2048]{1,0:T(8,128)(2,1)} %bitcast.12, bf16[2048,1536]{1,0:T(8,128)(2,1)} %bitcast.10), kind=kOutput, calls=%fused_computation.4 | convolution fusion | flops 3221225472 | bytes 10485760 | tf_op jit(solution)/shard_map/dot_general | solution.py:37
  227.1 30.7 %all-to-all-done = bf16[32,24,2048]{2,1,0:T(8,128)(2,1)} async-done(((bf16[32,24,2048]{2,1,0:T(8,128)(2,1)}), bf16[32,24,2048]{2,1,0:T(8,128)(2,1)}, u32[]{:S(2)}, u32[]{:S(2)}) %all-to-all-start) | async-done | bytes 3145760 | tf_op jit(solution)/shard_map/all_to_all | solution.py:55
  257.8 5.9 %multiply_convert_fusion.2 = (bf16[768,512]{0,1:T(8,128)(2,1)S(1)}, bf16[768,512]{0,1:T(8,128)(2,1)S(1)}) fusion(f32[768,1024]{0,1:T(8,128)} %fusion.2, bf16[768,2048]{1,0:T(8,128)(2,1)} %bitcast.5, bf16[2048,1536]{1,0:T(8,128)(2,1)} %bitcast.10), kind=kOutput, calls=%fused_computation.17 | convolution fusion | flops 1615724544 | bytes 9961472 | tf_op jit(solution)/shard_map/dot_general | solution.py:37
  263.7 3.9 %convolution_convert_fusion.3 = bf16[2048,512]{1,0:T(8,128)(2,1)S(1)} fusion(bf16[768,2048]{1,0:T(8,128)(2,1)} %bitcast.5, f32[768,1024]{0,1:T(8,128)S(1)} %copy-done.7), kind=kOutput, calls=%fused_computation.9 | convolution fusion | flops 1614020608 | bytes 8388608 | tf_op jit(solution)/shard_map/dot_general | solution.py:37
  267.6 6.7 %convolution_convert_fusion = bf16[2048,1024]{1,0:T(8,128)(2,1)S(1)} fusion(bf16[768,2048]{1,0:T(8,128)(2,1)} %bitcast.12, bf16[768,512]{0,1:T(8,128)(2,1)S(1)} %get-tuple-element.21, bf16[768,512]{0,1:T(8,128)(2,1)S(1)} %get-tuple-element.20), kind=kOutput, calls=%fused_computation.1 | convolution fusion | flops 3226468352 | bytes 8912896 | tf_op jit(solution)/shard_map/dot_general | solution.py:37
  274.3 3.2 pad_maximum_fusion
  277.5 0.0 reduce-scatter.2.cloned.1.call-update
  277.6 6.0 %fusion.4 = bf16[768,2048]{1,0:T(8,128)(2,1)S(1)} fusion(bf16[2048,1536]{1,0:T(8,128)(2,1)} %bitcast.10, bf16[768,512]{0,1:T(8,128)(2,1)S(1)} %get-tuple-element.21, bf16[768,512]{0,1:T(8,128)(2,1)S(1)} %get-tuple-element.20), kind=kOutput, calls=%fused_computation.6 | convolution fusion | flops 3225944064 | bytes 8912896 | tf_op jit(solution)/shard_map/dot_general | solution.py:37
  283.6 45.3 %all_to_all.20 = bf16[32,24,2048]{2,1,0:T(8,128)(2,1)S(1)} all-to-all(bf16[32,24,2048]{2,1,0:T(8,128)(2,1)S(1)} %bitcast.46), channel_id=1, replica_groups=mesh['expert'=32,'dp'=8] {'expert'}, dimensions={0} | all-to-all | bytes 6291456 | tf_op jit(solution)/shard_map/all_to_all | solution.py:55
  328.8 1.4 fusion.7
  330.3 16.5 %reduce-scatter.2.cloned.1.call-done = bf16[256,1536]{1,0:T(8,128)(2,1)} async-done(((bf16[2048,1536]{1,0:T(8,128)(2,1)}), bf16[256,1536]{1,0:T(8,128)(2,1)}) %reduce-scatter.2.cloned.1.call-update) | async-done | bytes 786448 | tf_op jit(solution)/shard_map/reduce_scatter | solution.py:80
  346.8 2.0 slice_bitcast_fusion
  348.8 0.8 copy.43
  (16 shorter events, 0.0 us)
Async XLA Ops:
  7.2 1.2 copy-start
  11.0 8.8 %copy-start.2 = (bf16[1,512,256]{2,1,0:T(8,128)(2,1)S(1)}, bf16[1,512,256]{2,1,0:T(8,128)(2,1)}, u32[]{:S(2)}) copy-start(bf16[1,512,256]{2,1,0:T(8,128)(2,1)} %param.13) | copy-start | bytes 786436
  11.0 8.9 %copy-start.3 = (bf16[1,256,512]{2,1,0:T(8,128)(2,1)S(1)}, bf16[1,256,512]{2,1,0:T(8,128)(2,1)}, u32[]{:S(2)}) copy-start(bf16[1,256,512]{2,1,0:T(8,128)(2,1)} %param.12) | copy-start | bytes 786436
  11.0 8.9 %copy-start.4 = (bf16[1,256,512]{2,1,0:T(8,128)(2,1)S(1)}, bf16[1,256,512]{2,1,0:T(8,128)(2,1)}, u32[]{:S(2)}) copy-start(bf16[1,256,512]{2,1,0:T(8,128)(2,1)} %param.11) | copy-start | bytes 786436
  11.0 48.0 %all-to-all-start.2 = ((bf16[32,24,2048]{2,1,0:T(8,128)(2,1)}), bf16[32,24,2048]{2,1,0:T(8,128)(2,1)}, u32[]{:S(2)}, u32[]{:S(2)}) async-start(bf16[32,24,2048]{2,1,0:T(8,128)(2,1)} %bitcast.44), calls=%async_computation.2 | async-start | bytes 6291456 | tf_op jit(solution)/shard_map/all_to_all | solution.py:55
  62.1 8.3 %copy-start.6 = (bf16[128,4]{0,1:T(4,128)(2,1)S(1)}, bf16[128,4]{0,1:T(4,128)(2,1)}, u32[]{:S(2)}) copy-start(bf16[128,4]{0,1:T(4,128)(2,1)} %param.10) | copy-start | bytes 3076
  62.2 8.3 %copy-start.5 = (s32[128,4]{0,1:T(4,128)S(1)}, s32[128,4]{0,1:T(4,128)}, u32[]{:S(2)}) copy-start(s32[128,4]{0,1:T(4,128)} %param.9) | copy-start | bytes 6148
  62.2 8.5 %copy-start.1 = (bf16[128,2048]{1,0:T(8,128)(2,1)S(1)}, bf16[128,2048]{1,0:T(8,128)(2,1)}, u32[]{:S(2)}) copy-start(bf16[128,2048]{1,0:T(8,128)(2,1)} %param.8) | copy-start | bytes 1572868
  62.2 150.1 %all-to-all-start.1 = ((bf16[8,256,1536]{2,1,0:T(8,128)(2,1)}), bf16[8,256,1536]{2,1,0:T(8,128)(2,1)}, u32[]{:S(2)}, u32[]{:S(2)}) async-start(bf16[8,256,1536]{2,1,0:T(8,128)(2,1)} %stack.2), calls=%async_computation.1 | async-start | bytes 12582912 | tf_op jit(solution)/shard_map/all_to_all | solution.py:49
  212.3 45.5 %all-to-all-start = ((bf16[32,24,2048]{2,1,0:T(8,128)(2,1)}), bf16[32,24,2048]{2,1,0:T(8,128)(2,1)}, u32[]{:S(2)}, u32[]{:S(2)}) async-start(bf16[32,24,2048]{2,1,0:T(8,128)(2,1)} %bitcast.45), calls=%async_computation | async-start | bytes 6291456 | tf_op jit(solution)/shard_map/all_to_all | solution.py:55
  218.6 128.2 %reduce-scatter.2.cloned.1.call-start = ((), (), s32[]{:S(2)}) async-start(), calls=%async_computation.5 | async-start | bytes 7077888 | tf_op jit(solution)/shard_map/reduce_scatter | solution.py:80
  257.8 5.9 %copy-start.7 = (f32[768,1024]{0,1:T(8,128)S(1)}, f32[768,1024]{0,1:T(8,128)}, u32[]{:S(2)}) copy-start(f32[768,1024]{0,1:T(8,128)} %fusion.2) | copy-start | bytes 9437188
Sparse Core Ops, SparseCore 0:
  277.7 69.0 reduce-scatter.1
